TPU v7x, 128 devices: a whole 4x4x4 slice. The times are simulated.
128 devices in a mesh: lsec: 8 (over z, core), rsec: 16 (over y, x).
Axes of the slice: x: 4, y: 4, z: 4, core: 2. Of those that a mesh axis runs over, the one named last changes fastest.
Arguments:
- wavefunction: bfloat16 [8192, 8192], P('lsec', 'rsec'), may hold values from -6 to 6
- left_env: bfloat16 [16, 8192, 1024], P(None, 'lsec'), may hold values from -0.1875 to 0.1875
- right_env: bfloat16 [16, 8192, 512], P(None, 'rsec'), may hold values from -0.25 to 0.25
Outputs:
- hpsi: bfloat16 [8192, 8192], P('lsec', 'rsec')
All inputs are finite; a program needn't handle non-finite values.
Results may differ from a plain program's by a relative error of at most 0.0053.
Values may be sent and summed in bfloat16 or wider, within the bound.
A program may use at most 128 MiB of HBM per device.

v0:
```python
import jax
import jax.numpy as jnp
from jax import lax
from jax.sharding import PartitionSpec as P

channel_shifts = (0, 1, -1, 0)


def shifted(value, axis, steps):
    count = lax.axis_size(axis)
    first, last = (max(0, -steps), min(count, count - steps))
    return lax.ppermute(value, axis, [(source, source + steps) for source in range(first, last)])


def contract(left_block, moved, right_block):
    partial_sum = jnp.dot(left_block, moved, preferred_element_type=jnp.float32).astype(
        jnp.bfloat16
    )
    return jnp.dot(partial_sum, right_block, preferred_element_type=jnp.float32)


def shards(wavefunction, left_env, right_env):
    count = left_env.shape[0]
    from_above = shifted(wavefunction, "lsec", -1)
    from_below = shifted(wavefunction, "lsec", 1)
    total = jnp.zeros(wavefunction.shape, jnp.float32)
    for channel in range(count):
        if channel_shifts[channel % 4] == 0:
            total = total + contract(left_env[channel], wavefunction, right_env[channel])
    upper = [c for c in range(count) if channel_shifts[c % 4] == 1]
    lower = [c for c in range(count) if channel_shifts[c % 4] == -1]
    upper_sum = jnp.zeros(wavefunction.shape, jnp.float32)
    for channel in upper:
        upper_sum = upper_sum + contract(left_env[channel], from_above, right_env[channel])
    lower_sum = jnp.zeros(wavefunction.shape, jnp.float32)
    for channel in lower:
        lower_sum = lower_sum + contract(left_env[channel], from_below, right_env[channel])
    upper_moved = shifted(upper_sum.astype(jnp.bfloat16), "rsec", -1)
    lower_moved = shifted(lower_sum.astype(jnp.bfloat16), "rsec", 1)
    total = total + upper_moved.astype(jnp.float32) + lower_moved.astype(jnp.float32)
    return total.astype(jnp.bfloat16)


def solution(mesh):
    in_specs = (P("lsec", "rsec"), P(None, "lsec", None), P(None, "rsec", None))
    out_specs = P("lsec", "rsec")
    return jax.shard_map(shards, mesh=mesh, in_specs=in_specs, out_specs=out_specs, check_vma=False)
```

profile of v0, /device:TPU:56, one launch (start us, length us, event | category | flops | bytes accessed | tf_op | source)
XLA Modules:
  0.0 111.7 jit_solution(13103006585519832573)
XLA Ops:
  0.0 0.0 copy-start
  0.0 2.0 %collective-permute-start.2 = (bf16[1024,512]{1,0:T(8,128)(2,1)}, bf16[1024,512]{1,0:T(8,128)(2,1)}, u32[]{:S(2)}, u32[]{:S(2)}) collective-permute-start(bf16[1024,512]{1,0:T(8,128)(2,1)} %param.3), channel_id=1, source_target_pairs={{0,16},{16,32},{32,48},{48,64},{64,80},{80,96},{96,112},{1,17},{17... | collective-permute-start | bytes 3145736 | tf_op jit(solution)/shard_map/ppermute | solution.py:12
  2.1 3.6 %collective-permute-start = (bf16[1024,512]{1,0:T(8,128)(2,1)}, bf16[1024,512]{1,0:T(8,128)(2,1)}, u32[]{:S(2)}, u32[]{:S(2)}) collective-permute-start(bf16[1024,512]{1,0:T(8,128)(2,1)} %param.3), channel_id=1, source_target_pairs={{16,0},{32,16},{48,32},{64,48},{80,64},{96,80},{112,96},{17,1},{33... | collective-permute-start | bytes 3145736 | tf_op jit(solution)/shard_map/ppermute | solution.py:12
  5.7 3.8 %fusion.115 = f32[1024,512]{1,0:T(8,128)S(1)} fusion(bf16[1024,512]{1,0:T(8,128)(2,1)} %param.3, bf16[16,1024,1024]{2,1,0:T(8,128)(2,1)} %param.4, bf16[16,512,512]{2,1,0:T(8,128)(2,1)} %param.5), kind=kOutput, calls=%fused_computation.73 | convolution fusion | flops 1611137024 | bytes 5767168 | tf_op jit(solution)/shard_map/dot_general | solution.py:19
  9.5 0.0 copy-done
  9.5 4.8 %fusion.118 = f32[1024,512]{1,0:T(8,128)} fusion(bf16[1024,512]{1,0:T(8,128)(2,1)S(1)} %copy-done, bf16[16,1024,1024]{2,1,0:T(8,128)(2,1)} %param.4, bf16[16,512,512]{2,1,0:T(8,128)(2,1)} %param.5), kind=kOutput, calls=%fused_computation.74 | convolution fusion | flops 1611137024 | bytes 5767168 | tf_op jit(solution)/shard_map/dot_general | solution.py:19
  14.3 4.8 %fusion.121 = f32[1024,512]{1,0:T(8,128)} fusion(bf16[1024,512]{1,0:T(8,128)(2,1)S(1)} %copy-done, bf16[16,1024,1024]{2,1,0:T(8,128)(2,1)} %param.4, bf16[16,512,512]{2,1,0:T(8,128)(2,1)} %param.5), kind=kOutput, calls=%fused_computation.75 | convolution fusion | flops 1611137024 | bytes 5767168 | tf_op jit(solution)/shard_map/dot_general | solution.py:19
  19.1 4.8 %fusion.124 = f32[1024,512]{1,0:T(8,128)} fusion(bf16[1024,512]{1,0:T(8,128)(2,1)S(1)} %copy-done, bf16[16,1024,1024]{2,1,0:T(8,128)(2,1)} %param.4, bf16[16,512,512]{2,1,0:T(8,128)(2,1)} %param.5), kind=kOutput, calls=%fused_computation.76 | convolution fusion | flops 1611137024 | bytes 5767168 | tf_op jit(solution)/shard_map/dot_general | solution.py:19
  23.8 0.0 collective-permute-done
  23.9 5.1 %fusion.106 = f32[1024,512]{1,0:T(8,128)} fusion(bf16[1024,512]{1,0:T(8,128)(2,1)} %collective-permute-done, bf16[16,1024,1024]{2,1,0:T(8,128)(2,1)} %param.4, bf16[16,512,512]{2,1,0:T(8,128)(2,1)} %param.5), kind=kOutput, calls=%fused_computation.70 | convolution fusion | flops 1611137024 | bytes 5767168 | tf_op jit(solution)/shard_map/dot_general | solution.py:19
  29.0 5.1 %fusion.109 = f32[1024,512]{1,0:T(8,128)} fusion(bf16[1024,512]{1,0:T(8,128)(2,1)} %collective-permute-done, bf16[16,1024,1024]{2,1,0:T(8,128)(2,1)} %param.4, bf16[16,512,512]{2,1,0:T(8,128)(2,1)} %param.5), kind=kOutput, calls=%fused_computation.71 | convolution fusion | flops 1611137024 | bytes 5767168 | tf_op jit(solution)/shard_map/dot_general | solution.py:19
  34.0 5.2 %fusion.112 = f32[1024,512]{1,0:T(8,128)} fusion(bf16[1024,512]{1,0:T(8,128)(2,1)} %collective-permute-done, bf16[16,1024,1024]{2,1,0:T(8,128)(2,1)} %param.4, bf16[16,512,512]{2,1,0:T(8,128)(2,1)} %param.5), kind=kOutput, calls=%fused_computation.72 | convolution fusion | flops 1611137024 | bytes 5767168 | tf_op jit(solution)/shard_map/dot_general | solution.py:19
  39.2 6.7 %add_convert_fusion.2 = bf16[1024,512]{1,0:T(8,128)(2,1)} fusion(f32[1024,512]{1,0:T(8,128)} %fusion.106, f32[1024,512]{1,0:T(8,128)} %fusion.112, f32[1024,512]{1,0:T(8,128)} %fusion.109, bf16[1024,512]{1,0:T(8,128)(2,1)} %collective-permute-done, bf16[16,1024,1024]{2,1,0:T(8,128)(2,1)} %param.4, bf16[16,512,512]{2,1,0:T(8,128)(2,1)} %param.5), kind=kOutput, calls=%fused_computation.38 | convolution fusion | flops 1613234176 | bytes 11010048 | tf_op jit(solution)/shard_map/dot_general | solution.py:19
  45.9 5.0 %collective-permute-start.1 = (bf16[1024,512]{1,0:T(8,128)(2,1)}, bf16[1024,512]{1,0:T(8,128)(2,1)}, u32[]{:S(2)}, u32[]{:S(2)}) collective-permute-start(bf16[1024,512]{1,0:T(8,128)(2,1)} %add_convert_fusion.2), channel_id=1, source_target_pairs={{1,0},{2,1},{3,2},{4,3},{5,4},{6,5},{7,6},{8,7},{9,8},{10,9},{11,1... | collective-permute-start | bytes 3145736 | tf_op jit(solution)/shard_map/ppermute | solution.py:12
  50.9 0.0 collective-permute-done.2
  50.9 5.1 %fusion.97 = f32[1024,512]{1,0:T(8,128)} fusion(bf16[1024,512]{1,0:T(8,128)(2,1)} %collective-permute-done.2, bf16[16,1024,1024]{2,1,0:T(8,128)(2,1)} %param.4, bf16[16,512,512]{2,1,0:T(8,128)(2,1)} %param.5), kind=kOutput, calls=%fused_computation.67 | convolution fusion | flops 1611137024 | bytes 5767168 | tf_op jit(solution)/shard_map/dot_general | solution.py:19
  56.1 5.1 %fusion.100 = f32[1024,512]{1,0:T(8,128)} fusion(bf16[1024,512]{1,0:T(8,128)(2,1)} %collective-permute-done.2, bf16[16,1024,1024]{2,1,0:T(8,128)(2,1)} %param.4, bf16[16,512,512]{2,1,0:T(8,128)(2,1)} %param.5), kind=kOutput, calls=%fused_computation.68 | convolution fusion | flops 1611137024 | bytes 5767168 | tf_op jit(solution)/shard_map/dot_general | solution.py:19
  61.2 5.1 %fusion.103 = f32[1024,512]{1,0:T(8,128)} fusion(bf16[1024,512]{1,0:T(8,128)(2,1)} %collective-permute-done.2, bf16[16,1024,1024]{2,1,0:T(8,128)(2,1)} %param.4, bf16[16,512,512]{2,1,0:T(8,128)(2,1)} %param.5), kind=kOutput, calls=%fused_computation.69 | convolution fusion | flops 1611137024 | bytes 5767168 | tf_op jit(solution)/shard_map/dot_general | solution.py:19
  66.3 6.7 %add_convert_fusion.1 = bf16[1024,512]{1,0:T(8,128)(2,1)} fusion(f32[1024,512]{1,0:T(8,128)} %fusion.97, f32[1024,512]{1,0:T(8,128)} %fusion.103, f32[1024,512]{1,0:T(8,128)} %fusion.100, bf16[1024,512]{1,0:T(8,128)(2,1)} %collective-permute-done.2, bf16[16,1024,1024]{2,1,0:T(8,128)(2,1)} %param.4, bf16[16,512,512]{2,1,0:T(8,128)(2,1)} %param.5), kind=kOutput, calls=%fused_computation.33 | convolution fusion | flops 1613234176 | bytes 11010048 | tf_op jit(solution)/shard_map/dot_general | solution.py:19
  73.0 1.9 %collective-permute-start.3 = (bf16[1024,512]{1,0:T(8,128)(2,1)}, bf16[1024,512]{1,0:T(8,128)(2,1)}, u32[]{:S(2)}, u32[]{:S(2)}) collective-permute-start(bf16[1024,512]{1,0:T(8,128)(2,1)} %add_convert_fusion.1), channel_id=1, source_target_pairs={{0,1},{1,2},{2,3},{3,4},{4,5},{5,6},{6,7},{7,8},{8,9},{9,10},{10,1... | collective-permute-start | bytes 3145736 | tf_op jit(solution)/shard_map/ppermute | solution.py:12
  74.9 4.8 %fusion.127 = f32[1024,512]{1,0:T(8,128)} fusion(bf16[1024,512]{1,0:T(8,128)(2,1)S(1)} %copy-done, bf16[16,1024,1024]{2,1,0:T(8,128)(2,1)} %param.4, bf16[16,512,512]{2,1,0:T(8,128)(2,1)} %param.5), kind=kOutput, calls=%fused_computation.77 | convolution fusion | flops 1611137024 | bytes 5767168 | tf_op jit(solution)/shard_map/dot_general | solution.py:19
  79.7 4.8 %fusion.130 = f32[1024,512]{1,0:T(8,128)} fusion(bf16[1024,512]{1,0:T(8,128)(2,1)S(1)} %copy-done, bf16[16,1024,1024]{2,1,0:T(8,128)(2,1)} %param.4, bf16[16,512,512]{2,1,0:T(8,128)(2,1)} %param.5), kind=kOutput, calls=%fused_computation.78 | convolution fusion | flops 1611137024 | bytes 5767168 | tf_op jit(solution)/shard_map/dot_general | solution.py:19
  84.5 4.8 %fusion.133 = f32[1024,512]{1,0:T(8,128)} fusion(bf16[1024,512]{1,0:T(8,128)(2,1)S(1)} %copy-done, bf16[16,1024,1024]{2,1,0:T(8,128)(2,1)} %param.4, bf16[16,512,512]{2,1,0:T(8,128)(2,1)} %param.5), kind=kOutput, calls=%fused_computation.79 | convolution fusion | flops 1611137024 | bytes 5767168 | tf_op jit(solution)/shard_map/dot_general | solution.py:19
  89.3 0.0 collective-permute-done.1
  89.3 13.1 %collective-permute-done.3 = bf16[1024,512]{1,0:T(8,128)(2,1)} collective-permute-done((bf16[1024,512]{1,0:T(8,128)(2,1)}, bf16[1024,512]{1,0:T(8,128)(2,1)}, u32[]{:S(2)}, u32[]{:S(2)}) %collective-permute-start.3) | collective-permute-done | bytes 1048608 | tf_op jit(solution)/shard_map/ppermute | solution.py:12
  102.4 9.3 %add_convert_fusion = bf16[1024,512]{1,0:T(8,128)(2,1)} fusion(bf16[1024,512]{1,0:T(8,128)(2,1)} %collective-permute-done.3, bf16[1024,512]{1,0:T(8,128)(2,1)} %collective-permute-done.1, f32[1024,512]{1,0:T(8,128)S(1)} %fusion.115, f32[1024,512]{1,0:T(8,128)} %fusion.118, f32[1024,512]{1,0:T(8,128)} %fusion.121, f32[1024,512]{1,0:T(8,128)} %fusion.124, ...), kind=kOutput, calls=%fused_computation.32 | convolution fusion | flops 1617428480 | bytes 21495808 | tf_op jit(solution)/shard_map/dot_general | solution.py:19
Async XLA Ops:
  0.0 9.5 %copy-start = (bf16[1024,512]{1,0:T(8,128)(2,1)S(1)}, bf16[1024,512]{1,0:T(8,128)(2,1)}, u32[]{:S(2)}) copy-start(bf16[1024,512]{1,0:T(8,128)(2,1)} %param.3) | copy-start | bytes 3145732
  0.0 50.9 %collective-permute-start.2 = (bf16[1024,512]{1,0:T(8,128)(2,1)}, bf16[1024,512]{1,0:T(8,128)(2,1)}, u32[]{:S(2)}, u32[]{:S(2)}) collective-permute-start(bf16[1024,512]{1,0:T(8,128)(2,1)} %param.3), channel_id=1, source_target_pairs={{0,16},{16,32},{32,48},{48,64},{64,80},{80,96},{96,112},{1,17},{17... | collective-permute-start | bytes 3145736 | tf_op jit(solution)/shard_map/ppermute | solution.py:12
  2.1 21.8 %collective-permute-start = (bf16[1024,512]{1,0:T(8,128)(2,1)}, bf16[1024,512]{1,0:T(8,128)(2,1)}, u32[]{:S(2)}, u32[]{:S(2)}) collective-permute-start(bf16[1024,512]{1,0:T(8,128)(2,1)} %param.3), channel_id=1, source_target_pairs={{16,0},{32,16},{48,32},{64,48},{80,64},{96,80},{112,96},{17,1},{33... | collective-permute-start | bytes 3145736 | tf_op jit(solution)/shard_map/ppermute | solution.py:12
  45.9 43.4 %collective-permute-start.1 = (bf16[1024,512]{1,0:T(8,128)(2,1)}, bf16[1024,512]{1,0:T(8,128)(2,1)}, u32[]{:S(2)}, u32[]{:S(2)}) collective-permute-start(bf16[1024,512]{1,0:T(8,128)(2,1)} %add_convert_fusion.2), channel_id=1, source_target_pairs={{1,0},{2,1},{3,2},{4,3},{5,4},{6,5},{7,6},{8,7},{9,8},{10,9},{11,1... | collective-permute-start | bytes 3145736 | tf_op jit(solution)/shard_map/ppermute | solution.py:12
  73.0 29.4 %collective-permute-start.3 = (bf16[1024,512]{1,0:T(8,128)(2,1)}, bf16[1024,512]{1,0:T(8,128)(2,1)}, u32[]{:S(2)}, u32[]{:S(2)}) collective-permute-start(bf16[1024,512]{1,0:T(8,128)(2,1)} %add_convert_fusion.1), channel_id=1, source_target_pairs={{0,1},{1,2},{2,3},{3,4},{4,5},{5,6},{6,7},{7,8},{8,9},{9,10},{10,1... | collective-permute-start | bytes 3145736 | tf_op jit(solution)/shard_map/ppermute | solution.py:12
where the time goes:
time: 112 us
  matrix products  85.9 us (77%)
  waiting for transfers between devices  13.1 us (12%)
  starting transfers between devices  12.6 us (11%)
    dot_general x16, matrix products, contract(): return jnp.dot(partial_sum, right_block, preferred_element_type=jnp.float32)  85.9 us
    ppermute x4, waiting for transfers between devices, shifted(): lax.ppermute(value, axis, [(source, source + steps) for source in range(f...  13.1 us
    ppermute x4, starting transfers between devices, shifted(): lax.ppermute(value, axis, [(source, source + steps) for source in range(f...  12.6 us
  transfers between devices with their start and end apart: 4, of which 1 were waited for; matrix products, arithmetic and copies ran while one was open for 69% of the time, Pallas kernels for 0%

commit v1 on v0

v1 whole, which is shorter than its diff:
```python
import functools

import jax
import jax.numpy as jnp
from jax import lax
from jax.experimental import pallas as pl
from jax.experimental.pallas import tpu as pltpu
from jax.sharding import PartitionSpec as P

MESH = pl.DeviceIdType.MESH
BF16 = jnp.bfloat16
F32 = jnp.float32

NEAR_ROWS = ((0, 256), (256, 256), (512, 512))
FAR_ROWS = ((0, 256), (256, 256), (512, 512))
LAST_ROWS = ((0, 512), (512, 512))


def dot(a, b):
    return jnp.dot(a, b, preferred_element_type=F32)


def kernel(
    n_i,
    n_j,
    psi_hbm,
    left_hbm,
    right_hbm,
    out_hbm,
    left,
    right,
    psi,
    part,
    total,
    term,
    arrived,
    result,
    psi_sem,
    left_sem,
    right_sem,
    psi_send,
    psi_recv,
    term_send,
    term_recv,
    out_sem,
):
    i, j = lax.axis_index("lsec"), lax.axis_index("rsec")
    odd = lax.rem(i, 2)
    near_i, far_i = i + 1 - 2 * odd, i - 1 + 2 * odd
    near_j, far_j = j - 1 + 2 * odd, j + 1 - 2 * odd
    has_far = jnp.logical_and(far_i >= 0, far_i < n_i)
    has_near_j = jnp.logical_and(near_j >= 0, near_j < n_j)
    has_far_j = jnp.logical_and(far_j >= 0, far_j < n_j)
    far_out = jnp.logical_and(has_far, has_far_j)
    far_in = jnp.logical_and(has_far, has_near_j)

    def channel(slot):
        if slot < 4:
            return 4 * slot + 1 + odd
        if slot < 8:
            return 4 * (slot - 4) + 2 - odd
        return 4 * ((slot - 8) // 2) + 3 * ((slot - 8) % 2)

    def load(slot):
        c = channel(slot)
        return (
            pltpu.make_async_copy(left_hbm.at[c], left.at[slot], left_sem.at[slot]),
            pltpu.make_async_copy(
                right_hbm.at[c], right.at[pl.ds(slot * 512, 512)], right_sem.at[slot]
            ),
        )

    def start(slots):
        for slot in slots:
            for copy in load(slot):
                copy.start()

    def await_(slots):
        for slot in slots:
            for copy in load(slot):
                copy.wait()

    own = pltpu.make_async_copy(psi_hbm, psi.at[0], psi_sem)
    own.start()
    start((8, 9))

    barrier = pltpu.get_barrier_semaphore()

    def greet(exists, device):
        @pl.when(exists)
        def _():
            pl.semaphore_signal(
                barrier, inc=1, device_id=device, device_id_type=MESH
            )

    pl.semaphore_signal(barrier, inc=1, device_id=(near_i, j), device_id_type=MESH)
    greet(has_far, (far_i, j))
    greet(has_near_j, (i, near_j))
    greet(has_far_j, (i, far_j))
    peers = 1 + sum(e.astype(jnp.int32) for e in (has_far, has_near_j, has_far_j))
    pl.semaphore_wait(barrier, peers)

    def psi_copy(k, device):
        return pltpu.make_async_remote_copy(
            src_ref=psi_hbm,
            dst_ref=psi.at[k],
            send_sem=psi_send.at[k - 1],
            recv_sem=psi_recv.at[k - 1],
            device_id=device,
            device_id_type=MESH,
        )

    near_psi = psi_copy(1, (near_i, j))
    far_psi = psi_copy(2, (far_i, j))
    near_psi.start()

    @pl.when(has_far)
    def _():
        far_psi.start()

    start((0, 1, 2, 3))

    def term_copy(k, at, rows, device):
        return pltpu.make_async_remote_copy(
            src_ref=term.at[k, pl.ds(*rows)],
            dst_ref=arrived.at[k, pl.ds(*rows)],
            send_sem=term_send.at[k, at],
            recv_sem=term_recv.at[k, at],
            device_id=device,
            device_id_type=MESH,
        )

    near_terms = [term_copy(0, a, r, (i, near_j)) for a, r in enumerate(NEAR_ROWS)]
    far_terms = [term_copy(1, a, r, (i, far_j)) for a, r in enumerate(FAR_ROWS)]

    def contract(slots, which, rows):
        first, size = rows
        for at, slot in enumerate(slots):
            part[pl.ds(0, size), at * 512 : (at + 1) * 512] = dot(
                left[slot, pl.ds(first, size), :], psi[which]
            ).astype(BF16)
        return dot(
            part[pl.ds(0, size), : len(slots) * 512],
            right[slots[0] * 512 : (slots[0] + len(slots)) * 512, :],
        )

    own.wait()
    await_((8, 9))
    total[...] = contract((8, 9), 0, (0, 1024))
    start((10, 11, 4, 5, 6, 7))

    near_psi.wait_recv()
    await_((0, 1, 2, 3))

    @pl.when(has_near_j)
    def _():
        for copy, rows in zip(near_terms, NEAR_ROWS):
            term[0, pl.ds(*rows), :] = contract((0, 1, 2, 3), 1, rows).astype(BF16)
            copy.start()

    start((12, 13, 14, 15))
    await_((10, 11))
    total[...] += contract((10, 11), 0, (0, 1024))

    await_((4, 5, 6, 7))

    @pl.when(has_far)
    def _():
        far_psi.wait_recv()

    @pl.when(far_out)
    def _():
        for copy, rows in zip(far_terms, FAR_ROWS):
            term[1, pl.ds(*rows), :] = contract((4, 5, 6, 7), 2, rows).astype(BF16)
            copy.start()

    @pl.when(jnp.logical_not(has_far_j))
    def _():
        arrived[0] = jnp.zeros((1024, 512), BF16)

    @pl.when(jnp.logical_not(far_in))
    def _():
        arrived[1] = jnp.zeros((1024, 512), BF16)

    await_((12, 13, 14, 15))
    for rows in LAST_ROWS:
        total[pl.ds(*rows), :] += contract((12, 13, 14, 15), 0, rows)

    written = []
    for at, rows in enumerate(NEAR_ROWS):

        @pl.when(has_far_j)
        def _(copy=near_terms[at]):
            copy.wait_recv()

        @pl.when(far_in)
        def _(copy=far_terms[at]):
            copy.wait_recv()

        here = pl.ds(*rows)
        result[here, :] = (
            total[here, :] + arrived[0, here, :].astype(F32) + arrived[1, here, :].astype(F32)
        ).astype(BF16)
        copy = pltpu.make_async_copy(result.at[here], out_hbm.at[here], out_sem.at[at])
        copy.start()
        written.append(copy)

    near_psi.wait_send()

    @pl.when(has_far)
    def _():
        far_psi.wait_send()

    @pl.when(has_near_j)
    def _():
        for copy in near_terms:
            copy.wait_send()

    @pl.when(far_out)
    def _():
        for copy in far_terms:
            copy.wait_send()

    for copy in written:
        copy.wait()


def solution(mesh):
    n_i, n_j = mesh.shape["lsec"], mesh.shape["rsec"]

    def shards(wavefunction, left_env, right_env):
        count, rows = left_env.shape[:2]
        columns = right_env.shape[1]
        any_space = pl.BlockSpec(memory_space=pl.ANY)
        return pl.pallas_call(
            functools.partial(kernel, n_i, n_j),
            out_shape=jax.ShapeDtypeStruct((rows, columns), BF16),
            in_specs=[any_space] * 3,
            out_specs=any_space,
            scratch_shapes=[
                pltpu.VMEM((count, rows, rows), BF16),
                pltpu.VMEM((count * columns, columns), BF16),
                pltpu.VMEM((3, rows, columns), BF16),
                pltpu.VMEM((rows, 4 * columns), BF16),
                pltpu.VMEM((rows, columns), F32),
                pltpu.VMEM((2, rows, columns), BF16),
                pltpu.VMEM((2, rows, columns), BF16),
                pltpu.VMEM((rows, columns), BF16),
                pltpu.SemaphoreType.DMA,
                pltpu.SemaphoreType.DMA((count,)),
                pltpu.SemaphoreType.DMA((count,)),
                pltpu.SemaphoreType.DMA((2,)),
                pltpu.SemaphoreType.DMA((2,)),
                pltpu.SemaphoreType.DMA((2, len(NEAR_ROWS))),
                pltpu.SemaphoreType.DMA((2, len(NEAR_ROWS))),
                pltpu.SemaphoreType.DMA((len(NEAR_ROWS),)),
            ],
            compiler_params=pltpu.CompilerParams(
                collective_id=0, has_side_effects=True, vmem_limit_bytes=62 << 20
            ),
        )(wavefunction, left_env, right_env)

    return jax.shard_map(
        shards,
        mesh=mesh,
        in_specs=(P("lsec", "rsec"), P(None, "lsec", None), P(None, "rsec", None)),
        out_specs=P("lsec", "rsec"),
        check_vma=False,
    )
```

time: 112 us -> 38.2 us (0.34)
  matrix products: 85.9 us -> 0 us
  Pallas kernels: 0 us -> 35.7 us
  waiting for transfers between devices: 13.1 us -> 0 us
  starting transfers between devices: 12.6 us -> 0 us
  local copies, waits for them, and re-layouts: 0.01 us -> 2.26 us
    dot_general x16 -> x0, matrix products: 85.9 us -> none  [contract(): return jnp.dot(partial_sum, right_block, preferred_element_type=jnp.float32)]
    pallas_call x0 -> x1, Pallas kernels: none -> 35.7 us  [shards(): pl.pallas_call(functools.partial(kernel, n_i, n_j), out_shape=jax.ShapeDt...]
    ppermute x4 -> x0, waiting for transfers between devices: 13.1 us -> none  [shifted(): lax.ppermute(value, axis, [(source, source + steps) for source in range(f...]
    ppermute x4 -> x0, starting transfers between devices: 12.6 us -> none  [shifted(): lax.ppermute(value, axis, [(source, source + steps) for source in range(f...]
    unnamed x2 -> x1, local copies, waits for them, and re-layouts: 0.01 us -> 2.26 us
  transfers between devices with their start and end apart: 4 -> 0, of which waited for: 1 -> 0; matrix products, arithmetic and copies ran while one was open for 69% -> 0% of each run, Pallas kernels for 0% -> 0%
where the time goes in v1:
time: 38.2 us; the launch traced here: 38 us
  Pallas kernels  35.7 us (93%)
  local copies, waits for them, and re-layouts  2.26 us (6%)
    pallas_call x1, Pallas kernels, shards(): pl.pallas_call(functools.partial(kernel, n_i, n_j), out_shape=jax.ShapeDt...  35.7 us
    unnamed x1, local copies, waits for them, and re-layouts  2.26 us

profile of v1, /device:TPU:56, one launch (start us, length us, event | category | flops | bytes accessed | tf_op | source)
XLA Modules:
  0.0 38.0 jit_solution(10730280264942478083)
XLA Ops:
  0.0 35.7 %shard_map.37 = bf16[1024,512]{1,0:T(8,128)(2,1)} custom-call(bf16[1024,512]{1,0:T(8,128)(2,1)} %psi_hbm.1, bf16[16,1024,1024]{2,1,0:T(8,128)(2,1)} %left_hbm.1, bf16[16,512,512]{2,1,0:T(8,128)(2,1)} %right_hbm.1), custom_call_target="tpu_custom_call" | custom-call | tf_op jit(solution)/shard_map/pallas_call | solution.py:235
  35.8 2.3 %copy.5 = bf16[1024,512]{1,0:T(8,128)(2,1)} copy(bf16[1024,512]{1,0:T(8,128)(2,1)} %shard_map.37) | data formatting | bytes 2097152

commit v2 on v1

v2 whole, which is shorter than its diff:
```python
import functools

import jax
import jax.numpy as jnp
from jax import lax
from jax.experimental import pallas as pl
from jax.experimental.pallas import tpu as pltpu
from jax.sharding import PartitionSpec as P

MESH = pl.DeviceIdType.MESH
BF16 = jnp.bfloat16
F32 = jnp.float32

TERM_ROWS = ((0, 256), (256, 256), (512, 512))
NEAR_PIECES = ((0, 512), (512, 512))
FAR_PIECES = ((0, 768), (768, 256))
LAST_ROWS = ((0, 512), (512, 512))


def dot(a, b):
    return jnp.dot(a, b, preferred_element_type=F32)


def kernel(
    n_i,
    n_j,
    psi_hbm,
    left_hbm,
    right_hbm,
    out_hbm,
    left,
    right,
    psi,
    part,
    sums,
    total,
    term,
    arrived,
    psi_sem,
    left_sem,
    rows_sem,
    right_sem,
    psi_send,
    psi_recv,
    term_send,
    term_recv,
):
    i, j = lax.axis_index("lsec"), lax.axis_index("rsec")
    odd = lax.rem(i, 2)
    near_i, far_i = i + 1 - 2 * odd, i - 1 + 2 * odd
    near_j, far_j = j - 1 + 2 * odd, j + 1 - 2 * odd
    has_far = jnp.logical_and(far_i >= 0, far_i < n_i)
    has_near_j = jnp.logical_and(near_j >= 0, near_j < n_j)
    has_far_j = jnp.logical_and(far_j >= 0, far_j < n_j)
    far_out = jnp.logical_and(has_far, has_far_j)
    far_in = jnp.logical_and(has_far, has_near_j)

    def channel(slot):
        if slot < 4:
            return 4 * slot + 1 + odd
        if slot < 8:
            return 4 * (slot - 4) + 2 - odd
        return 4 * ((slot - 8) // 2) + 3 * ((slot - 8) % 2)

    def load_right(slot):
        return pltpu.make_async_copy(
            right_hbm.at[channel(slot)],
            right.at[pl.ds(slot * 512, 512)],
            right_sem.at[slot],
        )

    def load_rows(at):
        rows = pl.ds(*TERM_ROWS[at])
        return [
            pltpu.make_async_copy(
                left_hbm.at[channel(slot), rows],
                left.at[slot, rows],
                rows_sem.at[slot, at],
            )
            for slot in range(4)
        ]

    def load(slot):
        c = channel(slot)
        return (
            pltpu.make_async_copy(left_hbm.at[c], left.at[slot], left_sem.at[slot]),
            load_right(slot),
        )

    def start(slots):
        for slot in slots:
            for copy in load(slot):
                copy.start()

    def await_(slots):
        for slot in slots:
            for copy in load(slot):
                copy.wait()

    own = pltpu.make_async_copy(psi_hbm, psi.at[0], psi_sem)
    own.start()
    start((8,))
    for slot in range(4):
        load_right(slot).start()
    for at in range(1):
        for copy in load_rows(at):
            copy.start()

    barrier = pltpu.get_barrier_semaphore()

    def greet(exists, device):
        @pl.when(exists)
        def _():
            pl.semaphore_signal(
                barrier, inc=1, device_id=device, device_id_type=MESH
            )

    pl.semaphore_signal(barrier, inc=1, device_id=(near_i, j), device_id_type=MESH)
    greet(has_far, (far_i, j))
    greet(has_near_j, (i, near_j))
    greet(has_far_j, (i, far_j))
    peers = 1 + sum(e.astype(jnp.int32) for e in (has_far, has_near_j, has_far_j))
    pl.semaphore_wait(barrier, peers)

    def psi_copies(k, pieces, device):
        return [
            pltpu.make_async_remote_copy(
                src_ref=psi_hbm.at[pl.ds(*rows)],
                dst_ref=psi.at[k, pl.ds(*rows)],
                send_sem=psi_send.at[k - 1, at],
                recv_sem=psi_recv.at[k - 1, at],
                device_id=device,
                device_id_type=MESH,
            )
            for at, rows in enumerate(pieces)
        ]

    near_psi = psi_copies(1, NEAR_PIECES, (near_i, j))
    far_psi = psi_copies(2, FAR_PIECES, (far_i, j))
    for copy in near_psi:
        copy.start()

    @pl.when(has_far)
    def _():
        for copy in far_psi:
            copy.start()

    for at in range(1, len(TERM_ROWS)):
        for copy in load_rows(at):
            copy.start()

    def term_copy(k, at, rows, device):
        return pltpu.make_async_remote_copy(
            src_ref=term.at[k, pl.ds(*rows)],
            dst_ref=arrived.at[k, pl.ds(*rows)],
            send_sem=term_send.at[k, at],
            recv_sem=term_recv.at[k, at],
            device_id=device,
            device_id_type=MESH,
        )

    near_terms = [term_copy(0, a, r, (i, near_j)) for a, r in enumerate(TERM_ROWS)]
    far_terms = [term_copy(1, a, r, (i, far_j)) for a, r in enumerate(TERM_ROWS)]

    def contract(slots, which, rows):
        first, size = rows
        for at, slot in enumerate(slots):
            part[pl.ds(0, size), at * 512 : (at + 1) * 512] = dot(
                left[slot, pl.ds(first, size), :], psi[which]
            ).astype(BF16)
        return dot(
            part[pl.ds(0, size), : len(slots) * 512],
            right[slots[0] * 512 : (slots[0] + len(slots)) * 512, :],
        )

    def contract_arriving(slots, which, pieces, copies, rows):
        first, size = rows
        last = len(pieces) - 1
        for piece, (depth_first, depth) in enumerate(pieces):
            copies[piece].wait_recv()
            for at, slot in enumerate(slots):
                here = slice(at * 512, (at + 1) * 512)
                value = dot(
                    left[slot, pl.ds(first, size), depth_first : depth_first + depth],
                    psi[which, pl.ds(depth_first, depth), :],
                )
                if piece:
                    value = value + sums[pl.ds(0, size), here]
                if piece < last:
                    sums[pl.ds(0, size), here] = value
                else:
                    part[pl.ds(0, size), here] = value.astype(BF16)
        return dot(
            part[pl.ds(0, size), : len(slots) * 512],
            right[slots[0] * 512 : (slots[0] + len(slots)) * 512, :],
        )

    own.wait()
    await_((8,))
    total[...] = contract((8,), 0, (0, 1024))

    for slot in range(4):
        load_right(slot).wait()
    later = ((9, 10), (4, 5), (6, 7), ())
    for at, rows in enumerate(TERM_ROWS):
        for copy in load_rows(at):
            copy.wait()

        @pl.when(has_near_j)
        def _(at=at, rows=rows):
            slots = (0, 1, 2, 3)
            if at:
                value = contract(slots, 1, rows)
            else:
                value = contract_arriving(slots, 1, NEAR_PIECES, near_psi, rows)
            term[0, pl.ds(*rows), :] = value.astype(BF16)
            near_terms[at].start()

        start(later[at])

    @pl.when(jnp.logical_not(has_near_j))
    def _():
        for copy in near_psi:
            copy.wait_recv()

    start((11, 12, 13, 14, 15))
    await_((9, 10))
    total[...] += contract((9, 10), 0, (0, 1024))

    await_((4, 5, 6, 7))

    @pl.when(far_out)
    def _():
        slots = (4, 5, 6, 7)
        for at, rows in enumerate(TERM_ROWS):
            if at:
                value = contract(slots, 2, rows)
            else:
                value = contract_arriving(slots, 2, FAR_PIECES, far_psi, rows)
            term[1, pl.ds(*rows), :] = value.astype(BF16)
            far_terms[at].start()

    @pl.when(jnp.logical_and(has_far, jnp.logical_not(has_far_j)))
    def _():
        for copy in far_psi:
            copy.wait_recv()

    @pl.when(jnp.logical_not(has_far_j))
    def _():
        arrived[0] = jnp.zeros((1024, 512), BF16)

    @pl.when(jnp.logical_not(far_in))
    def _():
        arrived[1] = jnp.zeros((1024, 512), BF16)

    await_((11, 12, 13, 14, 15))
    for rows in LAST_ROWS:
        total[pl.ds(*rows), :] += contract((11, 12, 13, 14, 15), 0, rows)

    for at, rows in enumerate(TERM_ROWS):

        @pl.when(has_far_j)
        def _(copy=near_terms[at]):
            copy.wait_recv()

        @pl.when(far_in)
        def _(copy=far_terms[at]):
            copy.wait_recv()

        here = pl.ds(*rows)
        out_hbm[here, :] = (
            total[here, :] + arrived[0, here, :].astype(F32) + arrived[1, here, :].astype(F32)
        ).astype(BF16)

    for copy in near_psi:
        copy.wait_send()

    @pl.when(has_far)
    def _():
        for copy in far_psi:
            copy.wait_send()

    @pl.when(has_near_j)
    def _():
        for copy in near_terms:
            copy.wait_send()

    @pl.when(far_out)
    def _():
        for copy in far_terms:
            copy.wait_send()


def solution(mesh):
    n_i, n_j = mesh.shape["lsec"], mesh.shape["rsec"]

    def shards(wavefunction, left_env, right_env):
        count, rows = left_env.shape[:2]
        columns = right_env.shape[1]
        any_space = pl.BlockSpec(memory_space=pl.ANY)
        return pl.pallas_call(
            functools.partial(kernel, n_i, n_j),
            out_shape=pltpu.VMEM((rows, columns), BF16),
            in_specs=[any_space] * 3,
            out_specs=pl.BlockSpec(memory_space=pltpu.VMEM),
            scratch_shapes=[
                pltpu.VMEM((count, rows, rows), BF16),
                pltpu.VMEM((count * columns, columns), BF16),
                pltpu.VMEM((3, rows, columns), BF16),
                pltpu.VMEM((rows, 5 * columns), BF16),
                pltpu.VMEM((TERM_ROWS[0][1], 4 * columns), F32),
                pltpu.VMEM((rows, columns), F32),
                pltpu.VMEM((2, rows, columns), BF16),
                pltpu.VMEM((2, rows, columns), BF16),
                pltpu.SemaphoreType.DMA,
                pltpu.SemaphoreType.DMA((count,)),
                pltpu.SemaphoreType.DMA((4, len(TERM_ROWS))),
                pltpu.SemaphoreType.DMA((count,)),
                pltpu.SemaphoreType.DMA((2, 2)),
                pltpu.SemaphoreType.DMA((2, 2)),
                pltpu.SemaphoreType.DMA((2, len(TERM_ROWS))),
                pltpu.SemaphoreType.DMA((2, len(TERM_ROWS))),
            ],
            compiler_params=pltpu.CompilerParams(
                collective_id=0, has_side_effects=True, vmem_limit_bytes=60 << 20
            ),
        )(wavefunction, left_env, right_env)

    return jax.shard_map(
        shards,
        mesh=mesh,
        in_specs=(P("lsec", "rsec"), P(None, "lsec", None), P(None, "rsec", None)),
        out_specs=P("lsec", "rsec"),
        check_vma=False,
    )
```

time: 38.2 us -> 35.1 us (0.919)
  Pallas kernels: 35.7 us -> 34 us
  local copies, waits for them, and re-layouts: 2.26 us -> 0.97 us
    pallas_call x1, Pallas kernels: 35.7 us -> 34 us  [shards(): pl.pallas_call(functools.partial(kernel, n_i, n_j), out_shape=pltpu.VMEM(...]
    unnamed x1, local copies, waits for them, and re-layouts: 2.26 us -> 0.97 us
where the time goes in v2:
time: 35.1 us; the launch traced here: 35 us
  Pallas kernels  34 us (97%)
  local copies, waits for them, and re-layouts  0.97 us (3%)
    pallas_call x1, Pallas kernels, shards(): pl.pallas_call(functools.partial(kernel, n_i, n_j), out_shape=pltpu.VMEM(...  34 us
    unnamed x1, local copies, waits for them, and re-layouts  0.97 us

profile of v2, /device:TPU:56, one launch (start us, length us, event | category | flops | bytes accessed | tf_op | source)
XLA Modules:
  0.0 35.0 jit_solution(2957310742635884536)
XLA Ops:
  0.0 34.0 %shard_map.37 = bf16[1024,512]{1,0:T(8,128)(2,1)S(1)} custom-call(bf16[1024,512]{1,0:T(8,128)(2,1)} %psi_hbm.1, bf16[16,1024,1024]{2,1,0:T(8,128)(2,1)} %left_hbm.1, bf16[16,512,512]{2,1,0:T(8,128)(2,1)} %right_hbm.1), custom_call_target="tpu_custom_call" | custom-call | tf_op jit(solution)/shard_map/pallas_call | solution.py:301
  34.0 1.0 %copy.5 = bf16[1024,512]{1,0:T(8,128)(2,1)} copy(bf16[1024,512]{1,0:T(8,128)(2,1)S(1)} %shard_map.37) | data formatting | bytes 2097152

commit v3 on v2

--- a/solution.py
+++ b/solution.py
@@ -12,7 +12,7 @@
 F32 = jnp.float32
 
 TERM_ROWS = ((0, 256), (256, 256), (512, 512))
-NEAR_PIECES = ((0, 512), (512, 512))
+NEAR_PIECES = ((0, 768), (768, 256))
 FAR_PIECES = ((0, 768), (768, 256))
 LAST_ROWS = ((0, 512), (512, 512))
 
@@ -55,6 +55,19 @@
     far_out = jnp.logical_and(has_far, has_far_j)
     far_in = jnp.logical_and(has_far, has_near_j)
 
+    barrier = pltpu.get_barrier_semaphore()
+
+    def greet(exists, device):
+        @pl.when(exists)
+        def _():
+            pl.semaphore_signal(
+                barrier, inc=1, device_id=device, device_id_type=MESH
+            )
+
+    pl.semaphore_signal(barrier, inc=1, device_id=(near_i, j), device_id_type=MESH)
+    greet(has_far, (far_i, j))
+    greet(has_near_j, (i, near_j))
+    greet(has_far_j, (i, far_j))
     def channel(slot):
         if slot < 4:
             return 4 * slot + 1 + odd
@@ -106,19 +119,6 @@
         for copy in load_rows(at):
             copy.start()
 
-    barrier = pltpu.get_barrier_semaphore()
-
-    def greet(exists, device):
-        @pl.when(exists)
-        def _():
-            pl.semaphore_signal(
-                barrier, inc=1, device_id=device, device_id_type=MESH
-            )
-
-    pl.semaphore_signal(barrier, inc=1, device_id=(near_i, j), device_id_type=MESH)
-    greet(has_far, (far_i, j))
-    greet(has_near_j, (i, near_j))
-    greet(has_far_j, (i, far_j))
     peers = 1 + sum(e.astype(jnp.int32) for e in (has_far, has_near_j, has_far_j))
     pl.semaphore_wait(barrier, peers)
 

time: 35.1 us -> 35.1 us (level)
  no operation moved by 1% of the time
where the time goes in v3:
time: 35.1 us; the launch traced here: 35 us
  Pallas kernels  34 us (97%)
  local copies, waits for them, and re-layouts  0.97 us (3%)
    pallas_call x1, Pallas kernels, shards(): pl.pallas_call(functools.partial(kernel, n_i, n_j), out_shape=pltpu.VMEM(...  34 us
    unnamed x1, local copies, waits for them, and re-layouts  0.97 us

profile of v3, /device:TPU:56, one launch (start us, length us, event | category | flops | bytes accessed | tf_op | source)
XLA Modules:
  0.0 35.0 jit_solution(7762551878279815269)
XLA Ops:
  0.0 34.0 %shard_map.37 = bf16[1024,512]{1,0:T(8,128)(2,1)S(1)} custom-call(bf16[1024,512]{1,0:T(8,128)(2,1)} %psi_hbm.1, bf16[16,1024,1024]{2,1,0:T(8,128)(2,1)} %left_hbm.1, bf16[16,512,512]{2,1,0:T(8,128)(2,1)} %right_hbm.1), custom_call_target="tpu_custom_call" | custom-call | tf_op jit(solution)/shard_map/pallas_call | solution.py:301
  34.0 1.0 %copy.5 = bf16[1024,512]{1,0:T(8,128)(2,1)} copy(bf16[1024,512]{1,0:T(8,128)(2,1)S(1)} %shard_map.37) | data formatting | bytes 2097152

commit v4 on v2

--- a/solution.py
+++ b/solution.py
@@ -11,10 +11,10 @@
 BF16 = jnp.bfloat16
 F32 = jnp.float32
 
-TERM_ROWS = ((0, 256), (256, 256), (512, 512))
+TERM_ROWS = ((0, 256), (256, 256), (512, 256), (768, 256))
 NEAR_PIECES = ((0, 512), (512, 512))
 FAR_PIECES = ((0, 768), (768, 256))
-LAST_ROWS = ((0, 512), (512, 512))
+LAST_ROWS = ((0, 1024),)
 
 
 def dot(a, b):
@@ -145,9 +145,6 @@
         for copy in far_psi:
             copy.start()
 
-    for at in range(1, len(TERM_ROWS)):
-        for copy in load_rows(at):
-            copy.start()
 
     def term_copy(k, at, rows, device):
         return pltpu.make_async_remote_copy(
@@ -198,6 +195,9 @@
     own.wait()
     await_((8,))
     total[...] = contract((8,), 0, (0, 1024))
+    for at in range(1, len(TERM_ROWS)):
+        for copy in load_rows(at):
+            copy.start()
 
     for slot in range(4):
         load_right(slot).wait()

time: 35.1 us -> 35.2 us (level)
  no operation moved by 1% of the time
where the time goes in v4:
time: 35.2 us; the launch traced here: 35.1 us
  Pallas kernels  34.2 us (97%)
  local copies, waits for them, and re-layouts  0.97 us (3%)
    pallas_call x1, Pallas kernels, shards(): pl.pallas_call(functools.partial(kernel, n_i, n_j), out_shape=pltpu.VMEM(...  34.2 us
    unnamed x1, local copies, waits for them, and re-layouts  0.97 us

profile of v4, /device:TPU:56, one launch (start us, length us, event | category | flops | bytes accessed | tf_op | source)
XLA Modules:
  0.0 35.1 jit_solution(2413998981917160205)
XLA Ops:
  0.0 34.2 %shard_map.37 = bf16[1024,512]{1,0:T(8,128)(2,1)S(1)} custom-call(bf16[1024,512]{1,0:T(8,128)(2,1)} %psi_hbm.1, bf16[16,1024,1024]{2,1,0:T(8,128)(2,1)} %left_hbm.1, bf16[16,512,512]{2,1,0:T(8,128)(2,1)} %right_hbm.1), custom_call_target="tpu_custom_call" | custom-call | tf_op jit(solution)/shard_map/pallas_call | solution.py:301
  34.2 1.0 %copy.5 = bf16[1024,512]{1,0:T(8,128)(2,1)} copy(bf16[1024,512]{1,0:T(8,128)(2,1)S(1)} %shard_map.37) | data formatting | bytes 2097152
